TPU v7x, 32 devices: a whole 2x2x4 slice. The times are simulated.
32 devices in a mesh: sec: 4 (over y, core), grp: 8 (over z, x).
Axes of the slice: x: 2, y: 2, z: 4, core: 2. Of those that a mesh axis runs over, the one named last changes fastest.
Arguments:
- solution_in: float32 [2, 32, 4, 6144], P(None, 'grp', None, 'sec'), may hold values from -6 to 6
- residual_in: float32 [2, 32, 4, 6144], P(None, 'grp', None, 'sec'), may hold values from -6 to 6
- direction_in: float32 [2, 32, 4, 6144], P(None, 'grp', None, 'sec'), may hold values from -6 to 6
- legendre: bfloat16 [32, 2, 128, 6144], P('grp', None, None, 'sec'), may hold values from -0.0034179688 to 0.0034179688
- inverse_prior: float32 [2, 6144], P(None, 'sec'), may hold values from 0.3 to 10
- noise_qq: float32 [128, 8192], P('grp', 'sec'), may hold values from 0.5 to 4
- noise_qu: float32 [128, 8192], P('grp', 'sec'), may hold values from -0.3 to 0.3
- noise_uu: float32 [128, 8192], P('grp', 'sec'), may hold values from 0.5 to 4
- pixel_mask: int32 [128, 8192], P('grp', 'sec'), may hold values 0 or 1
- cycle_phase: float32 [128], replicated, as said below
- m_values: int32 [32], replicated, may hold values from 0 to 6143, as said below
Outputs:
- solution: float32 [2, 32, 4, 6144], P(None, 'grp', None, 'sec')
- residual: float32 [2, 32, 4, 6144], P(None, 'grp', None, 'sec')
- direction: float32 [2, 32, 4, 6144], P(None, 'grp', None, 'sec')
Inputs may be any that keep to these rules, and one draw needn't show every extreme that they name: `m_values`: the slots' m values are distinct, and exactly one slot has m = 0. `cycle_phase`: each phase lies between 0 and 2 pi / 8192.
All inputs are finite; a program needn't handle non-finite values. No bound on the sum of `pixel_mask` on one device may be relied on, other than what follows from the above.
Results may differ from a plain program's by a relative error of at most 0.025.
Values sent between devices are 32-bit elements; how exact they have to be, the bound alone decides.
No kernel may reach another device: no remote copies, remote signals or barrier semaphores. Data moves between devices by JAX's collectives and lax.ppermute only.
A program may use at most 64 MiB of HBM per device.

v0:
```python
import math
import jax
import jax.numpy as jnp
from jax import lax
from jax.sharding import PartitionSpec as P

ITERS = 4
full_turn = 2.0 * math.pi


def combine_modes(prod):
    plus = prod[:, :, 0]
    minus = prod[:, :, 1]
    return jnp.stack(
        [
            -plus[:, :, 0] + minus[:, :, 3],
            -plus[:, :, 1] - minus[:, :, 2],
            -plus[:, :, 2] - minus[:, :, 1],
            -plus[:, :, 3] + minus[:, :, 0],
        ],
        axis=2,
    )


def adjoint_terms(field):
    half = field.astype(jnp.bfloat16)
    minus_part = jnp.stack([half[:, :, 3], -half[:, :, 2], -half[:, :, 1], half[:, :, 0]], axis=2)
    return jnp.stack([-half, minus_part], axis=2)


def legendre_forward(coeffs, legendre):
    half = coeffs.astype(jnp.bfloat16)
    prod = jnp.einsum("msrl,bmcl->bmscr", legendre, half, preferred_element_type=jnp.float32)
    return combine_modes(prod)


def legendre_adjoint(field, legendre):
    both = adjoint_terms(field)
    return jnp.einsum("msrl,bmscr->bmcl", legendre, both, preferred_element_type=jnp.float32)


def phi_table(m_values, start, count, total):
    index = start + jnp.arange(count, dtype=jnp.int32)
    folded = m_values[:, None] * index[None, :] % total
    angle = folded.astype(jnp.float32) * (full_turn / total)
    weight = jnp.where(m_values == 0, 1.0, 2.0).astype(jnp.float32)[:, None]
    return jnp.concatenate([weight * jnp.cos(angle), -weight * jnp.sin(angle)], axis=0)


def pixel_segment(field, cosines, sine_table, table, noise_qq, noise_qu, noise_uu, mask_f):
    count = field.shape[0]
    modes = field.shape[1]
    cycles = field.shape[3]
    parts = field.reshape(count, modes, 2, 2, cycles)
    real = parts[:, :, :, 0]
    imag = parts[:, :, :, 1]
    cosm = cosines[None, :, None, :]
    sinm = sine_table[None, :, None, :]
    rot_re = real * cosm - imag * sinm
    rot_im = real * sinm + imag * cosm
    rows = (
        jnp.stack([rot_re, rot_im], axis=1)
        .transpose(0, 3, 4, 1, 2)
        .reshape(count * 2 * cycles, 2 * modes)
    )
    pixels = jnp.dot(
        rows, table, precision=lax.Precision.HIGHEST, preferred_element_type=jnp.float32
    )
    pixels = pixels.reshape(count, 2, cycles, -1)
    qpart = pixels[:, 0]
    upart = pixels[:, 1]
    wq = mask_f * (noise_qq * qpart + noise_qu * upart)
    wu = mask_f * (noise_qu * qpart + noise_uu * upart)
    weighted = jnp.stack([wq, wu], axis=1).reshape(count * 2 * cycles, -1)
    back = jnp.dot(
        weighted, table.T, precision=lax.Precision.HIGHEST, preferred_element_type=jnp.float32
    )
    back = back.reshape(count, 2, cycles, 2, modes)
    out = jnp.stack([back[:, :, :, 0], back[:, :, :, 1]], axis=2)
    return out.transpose(0, 4, 1, 2, 3).reshape(count, modes, 4, cycles)


def rotate_back(field, cosines, sine_table):
    count = field.shape[0]
    modes = field.shape[1]
    cycles = field.shape[3]
    parts = field.reshape(count, modes, 2, 2, cycles)
    real = parts[:, :, :, 0]
    imag = parts[:, :, :, 1]
    cosm = cosines[None, :, None, :]
    sinm = sine_table[None, :, None, :]
    turned_real = real * cosm + imag * sinm
    turned_imag = imag * cosm - real * sinm
    return jnp.stack([turned_real, turned_imag], axis=3).reshape(count, modes, 4, cycles)


def totals(values):
    return jnp.sum(values, axis=(1, 2, 3))


def per_device(
    solution_in,
    residual_in,
    direction_in,
    legendre,
    inverse_prior,
    noise_qq,
    noise_qu,
    noise_uu,
    pixel_mask,
    cycle_phase,
    m_values,
):
    phi_local = noise_qq.shape[1]
    cycles_here = noise_qq.shape[0]
    modes_here = solution_in.shape[1]
    sections = lax.axis_size("sec")
    group_index = lax.axis_index("grp")
    local_phase = lax.dynamic_slice_in_dim(cycle_phase, group_index * cycles_here, cycles_here, 0)
    angle = m_values.astype(jnp.float32)[:, None] * local_phase[None, :]
    cosines = jnp.cos(angle)
    sine_table = jnp.sin(angle)
    local_m = lax.dynamic_slice_in_dim(m_values, group_index * modes_here, modes_here, 0)
    slot_angle = local_m.astype(jnp.float32)[:, None] * cycle_phase[None, :]
    slot_cos = jnp.cos(slot_angle)
    slot_sin = jnp.sin(slot_angle)
    mask_f = pixel_mask.astype(jnp.float32)
    prior = jnp.repeat(inverse_prior, 2, axis=0)[None, None]
    table = phi_table(m_values, lax.axis_index("sec") * phi_local, phi_local, phi_local * sections)
    solution, residual, direction = (solution_in, residual_in, direction_in)
    for step in range(ITERS):
        apply_field = legendre_forward(direction, legendre)
        field = lax.all_to_all(apply_field, "grp", split_axis=3, concat_axis=1, tiled=True)
        field = lax.psum(field, "sec")
        partial_field = pixel_segment(
            field, cosines, sine_table, table, noise_qq, noise_qu, noise_uu, mask_f
        )
        folded = lax.all_to_all(partial_field, "grp", split_axis=1, concat_axis=3, tiled=True)
        folded = lax.psum(folded, "sec")
        mode_field = rotate_back(folded, slot_cos, slot_sin)
        image = prior * direction + legendre_adjoint(mode_field, legendre)
        norm_now, curve, cross, square = lax.psum(
            (
                totals(residual * residual),
                totals(direction * image),
                totals(residual * image),
                totals(image * image),
            ),
            ("sec", "grp"),
        )
        step_size = norm_now / curve
        alpha = step_size[:, None, None, None]
        solution = solution + alpha * direction
        residual = residual - alpha * image
        norm_next = norm_now - 2.0 * step_size * cross + step_size * step_size * square
        direction = residual + (norm_next / norm_now)[:, None, None, None] * direction
    return (solution, residual, direction)


def solution(mesh):
    return jax.shard_map(
        per_device,
        mesh=mesh,
        in_specs=(
            P(None, "grp", None, "sec"),
            P(None, "grp", None, "sec"),
            P(None, "grp", None, "sec"),
            P("grp", None, None, "sec"),
            P(None, "sec"),
            P("grp", "sec"),
            P("grp", "sec"),
            P("grp", "sec"),
            P("grp", "sec"),
            P(),
            P(),
        ),
        out_specs=(
            P(None, "grp", None, "sec"),
            P(None, "grp", None, "sec"),
            P(None, "grp", None, "sec"),
        ),
        check_vma=False,
    )
```

profile of v0, /device:TPU:0, one launch (start us, length us, event | category | flops | bytes accessed | tf_op | source)
XLA Modules:
  0.0 451.1 jit_solution(6203677750327580794)
XLA Ops:
  5.5 2.4 reshape.484
  7.9 7.3 %all-to-all-start = ((f32[8,1,512]{2,1,0:T(1,128)}), f32[8,1,512]{2,1,0:T(1,128)S(1)}, u32[]{:S(2)}, u32[]{:S(2)}) async-start(f32[8,1,512]{2,1,0:T(1,128)} %reshape.484), calls=%async_computation | async-start | bytes 32768 | tf_op jit(solution)/shard_map/all_to_all | solution.py:133
  24.6 2.2 copy.135
  26.8 12.4 %psum.169 = f32[2,32,2,2,16]{4,1,3,2,0:T(8,128)} all-reduce(f32[2,32,2,2,16]{4,1,3,2,0:T(8,128)} %bitcast.348), channel_id=1, replica_groups=mesh['sec'=4,'grp'=8] {'sec'}, use_global_device_ids=true, to_apply=%region_2.3 | all-reduce | flops 4096 | bytes 32768 | tf_op jit(solution)/shard_map/psum | solution.py:134
  45.3 2.5 fusion.52
  50.2 4.5 all-to-all-start.1
  55.8 5.5 %all-to-all-done.1 = f32[8,1,512]{2,1,0:T(1,128)S(1)} async-done(((f32[8,1,512]{2,1,0:T(1,128)}), f32[8,1,512]{2,1,0:T(1,128)S(1)}, u32[]{:S(2)}, u32[]{:S(2)}) %all-to-all-start.1) | async-done | bytes 16416 | tf_op jit(solution)/shard_map/all_to_all | solution.py:138
  65.4 10.1 %psum.170 = f32[2,4,2,2,128]{4,3,2,1,0:T(2,128)S(1)} all-reduce(f32[2,4,2,2,128]{4,3,2,1,0:T(2,128)S(1)} %reshape.451), channel_id=1, replica_groups=mesh['sec'=4,'grp'=8] {'sec'}, use_global_device_ids=true, to_apply=%region_3.4 | all-reduce | flops 4096 | bytes 32768 | tf_op jit(solution)/shard_map/psum | solution.py:139
  75.6 2.2 multiply_reduce_fusion.12
  77.9 38.3 %all-reduce.3 = (f32[2]{0:T(128)S(1)}, f32[2]{0:T(128)S(1)}, f32[2]{0:T(128)S(1)}, f32[2]{0:T(128)S(1)}) all-reduce(f32[2]{0:T(128)S(1)} %multiply_reduce_fusion.15, f32[2]{0:T(128)S(1)} %get-tuple-element.29, f32[2]{0:T(128)S(1)} %get-tuple-element.28, f32[2]{0:T(128)S(1)} %get-tuple-element.27), channel_id=1, replica_groups=mesh['sec'=4,'grp'=8] {'sec','grp'}, use_global_device_ids=true, to_apply=%region_1.2 | all-reduce | flops 8 | bytes 64 | tf_op jit(solution)/shard_map/psum | solution.py:142
  122.7 10.9 %all_to_all.144 = f32[8,1,512]{2,1,0:T(1,128)S(1)} all-to-all(f32[8,1,512]{2,1,0:T(1,128)S(1)} %reshape.488), channel_id=1, replica_groups=mesh['sec'=4,'grp'=8] {'grp'}, dimensions={0} | all-to-all | bytes 32768 | tf_op jit(solution)/shard_map/all_to_all | solution.py:133
  135.9 2.2 copy.153
  139.7 12.6 %psum.175 = f32[2,32,2,2,16]{4,1,2,0,3:T(8,128)} all-reduce(f32[2,32,2,2,16]{4,1,2,0,3:T(8,128)} %copy.154), channel_id=1, replica_groups=mesh['sec'=4,'grp'=8] {'sec'}, use_global_device_ids=true, to_apply=%region_12.13 | all-reduce | flops 4096 | bytes 32768 | tf_op jit(solution)/shard_map/psum | solution.py:134
  158.4 2.5 fusion.55
  162.7 8.9 %all_to_all.145 = f32[8,1,512]{2,1,0:T(1,128)S(1)} all-to-all(f32[8,1,512]{2,1,0:T(1,128)S(1)} %reshape.490), channel_id=1, replica_groups=mesh['sec'=4,'grp'=8] {'grp'}, dimensions={0} | all-to-all | bytes 32768 | tf_op jit(solution)/shard_map/all_to_all | solution.py:138
  175.7 10.1 %psum.176 = f32[2,4,2,2,128]{4,3,2,1,0:T(2,128)S(1)} all-reduce(f32[2,4,2,2,128]{4,3,2,1,0:T(2,128)S(1)} %reshape.454), channel_id=1, replica_groups=mesh['sec'=4,'grp'=8] {'sec'}, use_global_device_ids=true, to_apply=%region_13.14 | all-reduce | flops 4096 | bytes 32768 | tf_op jit(solution)/shard_map/psum | solution.py:139
  186.0 2.2 multiply_reduce_fusion.8
  188.2 38.7 %all-reduce.2 = (f32[2]{0:T(128)S(1)}, f32[2]{0:T(128)S(1)}, f32[2]{0:T(128)S(1)}, f32[2]{0:T(128)S(1)}) all-reduce(f32[2]{0:T(128)S(1)} %get-tuple-element.26, f32[2]{0:T(128)S(1)} %get-tuple-element.25, f32[2]{0:T(128)S(1)} %get-tuple-element.24, f32[2]{0:T(128)S(1)} %get-tuple-element.23), channel_id=1, replica_groups=mesh['sec'=4,'grp'=8] {'sec','grp'}, use_global_device_ids=true, to_apply=%region_7.8 | all-reduce | flops 8 | bytes 64 | tf_op jit(solution)/shard_map/psum | solution.py:142
  233.4 10.9 %all_to_all.146 = f32[8,1,512]{2,1,0:T(1,128)S(1)} all-to-all(f32[8,1,512]{2,1,0:T(1,128)S(1)} %reshape.492), channel_id=1, replica_groups=mesh['sec'=4,'grp'=8] {'grp'}, dimensions={0} | all-to-all | bytes 32768 | tf_op jit(solution)/shard_map/all_to_all | solution.py:133
  250.4 12.4 %psum.181 = f32[2,32,2,2,16]{4,1,2,0,3:T(8,128)} all-reduce(f32[2,32,2,2,16]{4,1,2,0,3:T(8,128)} %copy.166), channel_id=1, replica_groups=mesh['sec'=4,'grp'=8] {'sec'}, use_global_device_ids=true, to_apply=%region_22.23 | all-reduce | flops 4096 | bytes 32768 | tf_op jit(solution)/shard_map/psum | solution.py:134
  268.9 2.5 fusion.58
  273.2 8.9 %all_to_all.147 = f32[8,1,512]{2,1,0:T(1,128)S(1)} all-to-all(f32[8,1,512]{2,1,0:T(1,128)S(1)} %reshape.494), channel_id=1, replica_groups=mesh['sec'=4,'grp'=8] {'grp'}, dimensions={0} | all-to-all | bytes 32768 | tf_op jit(solution)/shard_map/all_to_all | solution.py:138
  286.2 10.1 %psum.182 = f32[2,4,2,2,128]{4,3,2,1,0:T(2,128)S(1)} all-reduce(f32[2,4,2,2,128]{4,3,2,1,0:T(2,128)S(1)} %reshape.457), channel_id=1, replica_groups=mesh['sec'=4,'grp'=8] {'sec'}, use_global_device_ids=true, to_apply=%region_23.24 | all-reduce | flops 4096 | bytes 32768 | tf_op jit(solution)/shard_map/psum | solution.py:139
  296.5 2.2 multiply_reduce_fusion.4
  298.7 38.7 %all-reduce.1 = (f32[2]{0:T(128)S(1)}, f32[2]{0:T(128)S(1)}, f32[2]{0:T(128)S(1)}, f32[2]{0:T(128)S(1)}) all-reduce(f32[2]{0:T(128)S(1)} %get-tuple-element.22, f32[2]{0:T(128)S(1)} %get-tuple-element.21, f32[2]{0:T(128)S(1)} %get-tuple-element.20, f32[2]{0:T(128)S(1)} %get-tuple-element.19), channel_id=1, replica_groups=mesh['sec'=4,'grp'=8] {'sec','grp'}, use_global_device_ids=true, to_apply=%region_17.18 | all-reduce | flops 8 | bytes 64 | tf_op jit(solution)/shard_map/psum | solution.py:142
  344.0 10.9 %all_to_all.148 = f32[8,1,512]{2,1,0:T(1,128)S(1)} all-to-all(f32[8,1,512]{2,1,0:T(1,128)S(1)} %reshape.496), channel_id=1, replica_groups=mesh['sec'=4,'grp'=8] {'grp'}, dimensions={0} | all-to-all | bytes 32768 | tf_op jit(solution)/shard_map/all_to_all | solution.py:133
  361.0 12.4 %psum.187 = f32[2,32,2,2,16]{4,1,2,0,3:T(8,128)} all-reduce(f32[2,32,2,2,16]{4,1,2,0,3:T(8,128)} %copy.178), channel_id=1, replica_groups=mesh['sec'=4,'grp'=8] {'sec'}, use_global_device_ids=true, to_apply=%region_32.33 | all-reduce | flops 4096 | bytes 32768 | tf_op jit(solution)/shard_map/psum | solution.py:134
  378.8 2.5 fusion.61
  383.1 8.9 %all_to_all.149 = f32[8,1,512]{2,1,0:T(1,128)S(1)} all-to-all(f32[8,1,512]{2,1,0:T(1,128)S(1)} %reshape.498), channel_id=1, replica_groups=mesh['sec'=4,'grp'=8] {'grp'}, dimensions={0} | all-to-all | bytes 32768 | tf_op jit(solution)/shard_map/all_to_all | solution.py:138
  396.1 10.1 %psum.188 = f32[2,4,2,2,128]{4,3,2,1,0:T(2,128)S(1)} all-reduce(f32[2,4,2,2,128]{4,3,2,1,0:T(2,128)S(1)} %reshape.460), channel_id=1, replica_groups=mesh['sec'=4,'grp'=8] {'sec'}, use_global_device_ids=true, to_apply=%region_33.34 | all-reduce | flops 4096 | bytes 32768 | tf_op jit(solution)/shard_map/psum | solution.py:139
  406.4 2.2 multiply_reduce_fusion.1
  408.7 38.7 %all-reduce = (f32[2]{0:T(128)S(1)}, f32[2]{0:T(128)S(1)}, f32[2]{0:T(128)S(1)}, f32[2]{0:T(128)S(1)}) all-reduce(f32[2]{0:T(128)S(1)} %get-tuple-element.18, f32[2]{0:T(128)S(1)} %get-tuple-element.17, f32[2]{0:T(128)S(1)} %get-tuple-element.16, f32[2]{0:T(128)S(1)} %get-tuple-element.15), channel_id=1, replica_groups=mesh['sec'=4,'grp'=8] {'sec','grp'}, use_global_device_ids=true, to_apply=%region_27.28 | all-reduce | flops 8 | bytes 64 | tf_op jit(solution)/shard_map/psum | solution.py:142
  (168 shorter events, 102.4 us)
Async XLA Ops:
  0.6 1.9 copy-start
  0.6 14.5 %copy-start.7 = (s32[32]{0:T(128)S(1)}, s32[32]{0:T(128)}, u32[]{:S(2)}) copy-start(s32[32]{0:T(128)} %param.21) | copy-start | bytes 388
  0.7 14.6 %copy-start.8 = (f32[128]{0:T(128)S(1)}, f32[128]{0:T(128)}, u32[]{:S(2)}) copy-start(f32[128]{0:T(128)} %param.20) | copy-start | bytes 1540
  7.9 13.9 %all-to-all-start = ((f32[8,1,512]{2,1,0:T(1,128)}), f32[8,1,512]{2,1,0:T(1,128)S(1)}, u32[]{:S(2)}, u32[]{:S(2)}) async-start(f32[8,1,512]{2,1,0:T(1,128)} %reshape.484), calls=%async_computation | async-start | bytes 32768 | tf_op jit(solution)/shard_map/all_to_all | solution.py:133
  16.6 0.7 copy-start.1
  24.6 31.2 %copy-start.6 = (f32[2,1536]{1,0:T(2,128)S(1)}, f32[2,1536]{1,0:T(2,128)}, u32[]{:S(2)}) copy-start(f32[2,1536]{1,0:T(2,128)} %param.15) | copy-start | bytes 36868
  50.2 11.1 %all-to-all-start.1 = ((f32[8,1,512]{2,1,0:T(1,128)}), f32[8,1,512]{2,1,0:T(1,128)S(1)}, u32[]{:S(2)}, u32[]{:S(2)}) async-start(f32[8,1,512]{2,1,0:T(1,128)} %reshape.486), calls=%async_computation.1 | async-start | bytes 32768 | tf_op jit(solution)/shard_map/all_to_all | solution.py:138
  118.2 0.7 copy-start.2
  228.9 0.7 copy-start.4
  339.4 0.7 copy-start.5
  378.8 68.6 %copy-start.3 = (f32[2,4,4,1536]{3,2,0,1:T(4,128)S(1)}, f32[2,4,4,1536]{3,2,0,1:T(4,128)}, u32[]{:S(2)}) copy-start(f32[2,4,4,1536]{3,2,0,1:T(4,128)} %copy-done.2) | copy-start | bytes 589828
where the time goes:
time: 454 us; the launch traced here: 451 us
  blocking collectives  304 us (67%)
  local copies, waits for them, and re-layouts  67 us (15%)
  matrix products  29.7 us (7%)
  other arithmetic  29.5 us (6%)
  starting transfers between devices  11.8 us (3%)
  waiting for transfers between devices  7.35 us (2%)
    psum x4, blocking collectives, per_device(): lax.psum((totals(residual * residual), totals(direction * image), totals(...  155 us
    psum x4, blocking collectives, per_device(): field = lax.psum(field, 'sec')  49.9 us
    psum x4, blocking collectives, per_device(): folded = lax.psum(folded, 'sec')  40.5 us
    all_to_all x3, blocking collectives, per_device(): lax.all_to_all(apply_field, 'grp', split_axis=3, concat_axis=1, tiled=True)  32.7 us
    unnamed x37, local copies, waits for them, and re-layouts  28.9 us
    all_to_all x3, blocking collectives, per_device(): lax.all_to_all(partial_field, 'grp', split_axis=1, concat_axis=3, tiled=T...  26.8 us
    dot_general x4, matrix products, pixel_segment(): jnp.dot(weighted, table.T, precision=lax.Precision.HIGHEST, preferred_ele...  9.92 us
    all_to_all x5, local copies, waits for them, and re-layouts, per_device(): lax.all_to_all(apply_field, 'grp', split_axis=3, concat_axis=1, tiled=True)  9.38 us
  transfers between devices with their start and end apart: 2, of which 2 were waited for; matrix products, arithmetic and copies ran while one was open for 1% of the time, Pallas kernels for 0%

commit v1 on v0

--- a/solution.py
+++ b/solution.py
@@ -130,7 +130,12 @@
     solution, residual, direction = (solution_in, residual_in, direction_in)
     for step in range(ITERS):
         apply_field = legendre_forward(direction, legendre)
-        field = lax.all_to_all(apply_field, "grp", split_axis=3, concat_axis=1, tiled=True)
+        field = jnp.concatenate(
+            lax.all_to_all(
+                jnp.stack(jnp.split(apply_field, lax.axis_size("grp"), axis=3)), "grp", 0, 0
+            ),
+            axis=1,
+        )
         field = lax.psum(field, "sec")
         partial_field = pixel_segment(
             field, cosines, sine_table, table, noise_qq, noise_qu, noise_uu, mask_f

time: 454 us -> 426 us (0.938)
  local copies, waits for them, and re-layouts: 67 us -> 46.3 us
    all_to_all x5 -> x1, local copies, waits for them, and re-layouts: 9.38 us -> 0.54 us  [per_device(): lax.all_to_all(jnp.stack(jnp.split(apply_field, lax.axis_size('grp'), axi...]
    unnamed x37 -> x79, local copies, waits for them, and re-layouts: 28.9 us -> 25.8 us
where the time goes in v1:
time: 426 us; the launch traced here: 424 us
  blocking collectives  304 us (71%)
  local copies, waits for them, and re-layouts  46.3 us (11%)
  other arithmetic  26.7 us (6%)
  matrix products  25.6 us (6%)
  starting transfers between devices  11.8 us (3%)
  waiting for transfers between devices  7.34 us (2%)
    psum x4, blocking collectives, per_device(): lax.psum((totals(residual * residual), totals(direction * image), totals(...  155 us
    psum x4, blocking collectives, per_device(): field = lax.psum(field, 'sec')  49.7 us
    psum x4, blocking collectives, per_device(): folded = lax.psum(folded, 'sec')  40.6 us
    all_to_all x3, blocking collectives, per_device(): lax.all_to_all(jnp.stack(jnp.split(apply_field, lax.axis_size('grp'), axi...  32.7 us
    all_to_all x3, blocking collectives, per_device(): lax.all_to_all(partial_field, 'grp', split_axis=1, concat_axis=3, tiled=T...  26.8 us
    unnamed x79, local copies, waits for them, and re-layouts  25.8 us
    dot_general x4, matrix products, legendre_adjoint(): jnp.einsum('msrl,bmscr->bmcl', legendre, both, preferred_element_type=jnp...  8.97 us
  transfers between devices with their start and end apart: 2, of which 2 were waited for; matrix products, arithmetic and copies ran while one was open for 1% of the time, Pallas kernels for 0%

profile of v1, /device:TPU:0, one launch (start us, length us, event | category | flops | bytes accessed | tf_op | source)
XLA Modules:
  0.0 423.6 jit_solution(7066112032806029338)
XLA Ops:
  0.7 1.9 copy-done
  2.5 1.9 fusion.40
  5.8 7.3 %all-to-all-start = ((f32[8,1,512]{2,1,0:T(1,128)}), f32[8,1,512]{2,1,0:T(1,128)S(1)}, u32[]{:S(2)}, u32[]{:S(2)}) async-start(f32[8,1,512]{2,1,0:T(1,128)} %reshape.516), calls=%async_computation | async-start | bytes 32768 | tf_op jit(solution)/shard_map/all_to_all | solution.py:134
  17.8 1.9 all-to-all-done
  21.7 12.4 %psum.169 = f32[2,32,2,2,16]{4,3,2,0,1:T(2,128)} all-reduce(f32[2,32,2,2,16]{4,3,2,0,1:T(2,128)} %bitcast.462), channel_id=1, replica_groups=mesh['sec'=4,'grp'=8] {'sec'}, use_global_device_ids=true, to_apply=%region_2.3 | all-reduce | flops 4096 | bytes 32768 | tf_op jit(solution)/shard_map/psum | solution.py:139
  40.5 1.6 reshape.518
  42.1 4.5 %all-to-all-start.1 = ((f32[8,1,512]{2,1,0:T(1,128)}), f32[8,1,512]{2,1,0:T(1,128)S(1)}, u32[]{:S(2)}, u32[]{:S(2)}) async-start(f32[8,1,512]{2,1,0:T(1,128)} %reshape.518), calls=%async_computation.1 | async-start | bytes 32768 | tf_op jit(solution)/shard_map/all_to_all | solution.py:143
  47.7 5.5 %all-to-all-done.1 = f32[8,1,512]{2,1,0:T(1,128)S(1)} async-done(((f32[8,1,512]{2,1,0:T(1,128)}), f32[8,1,512]{2,1,0:T(1,128)S(1)}, u32[]{:S(2)}, u32[]{:S(2)}) %all-to-all-start.1) | async-done | bytes 16416 | tf_op jit(solution)/shard_map/all_to_all | solution.py:143
  57.3 10.1 %psum.170 = f32[2,4,2,2,128]{4,3,2,1,0:T(2,128)S(1)} all-reduce(f32[2,4,2,2,128]{4,3,2,1,0:T(2,128)S(1)} %reshape.477), channel_id=1, replica_groups=mesh['sec'=4,'grp'=8] {'sec'}, use_global_device_ids=true, to_apply=%region_3.4 | all-reduce | flops 4096 | bytes 32768 | tf_op jit(solution)/shard_map/psum | solution.py:144
  67.6 2.2 multiply_reduce_fusion.12
  69.8 38.3 %all-reduce.3 = (f32[2]{0:T(128)S(1)}, f32[2]{0:T(128)S(1)}, f32[2]{0:T(128)S(1)}, f32[2]{0:T(128)S(1)}) all-reduce(f32[2]{0:T(128)S(1)} %multiply_reduce_fusion.15, f32[2]{0:T(128)S(1)} %get-tuple-element.29, f32[2]{0:T(128)S(1)} %get-tuple-element.28, f32[2]{0:T(128)S(1)} %get-tuple-element.27), channel_id=1, replica_groups=mesh['sec'=4,'grp'=8] {'sec','grp'}, use_global_device_ids=true, to_apply=%region_1.2 | all-reduce | flops 8 | bytes 64 | tf_op jit(solution)/shard_map/psum | solution.py:147
  108.2 1.9 multiply_add_fusion.3
  114.2 10.9 %all_to_all.92 = f32[8,1,512]{2,1,0:T(1,128)S(1)} all-to-all(f32[8,1,512]{2,1,0:T(1,128)S(1)} %reshape.520), channel_id=1, replica_groups=mesh['sec'=4,'grp'=8] {'grp'}, dimensions={0} | all-to-all | bytes 32768 | tf_op jit(solution)/shard_map/all_to_all | solution.py:134
  128.2 12.4 %psum.175 = f32[2,32,2,2,16]{4,2,0,1,3:T(2,128)} all-reduce(f32[2,32,2,2,16]{4,2,0,1,3:T(2,128)} %copy.142), channel_id=1, replica_groups=mesh['sec'=4,'grp'=8] {'sec'}, use_global_device_ids=true, to_apply=%region_12.13 | all-reduce | flops 4096 | bytes 32768 | tf_op jit(solution)/shard_map/psum | solution.py:139
  147.8 8.9 %all_to_all.93 = f32[8,1,512]{2,1,0:T(1,128)S(1)} all-to-all(f32[8,1,512]{2,1,0:T(1,128)S(1)} %reshape.522), channel_id=1, replica_groups=mesh['sec'=4,'grp'=8] {'grp'}, dimensions={0} | all-to-all | bytes 32768 | tf_op jit(solution)/shard_map/all_to_all | solution.py:143
  160.8 10.3 %psum.176 = f32[2,4,2,2,128]{4,3,2,1,0:T(2,128)S(1)} all-reduce(f32[2,4,2,2,128]{4,3,2,1,0:T(2,128)S(1)} %reshape.482), channel_id=1, replica_groups=mesh['sec'=4,'grp'=8] {'sec'}, use_global_device_ids=true, to_apply=%region_13.14 | all-reduce | flops 4096 | bytes 32768 | tf_op jit(solution)/shard_map/psum | solution.py:144
  171.3 2.2 multiply_reduce_fusion.8
  173.5 38.7 %all-reduce.2 = (f32[2]{0:T(128)S(1)}, f32[2]{0:T(128)S(1)}, f32[2]{0:T(128)S(1)}, f32[2]{0:T(128)S(1)}) all-reduce(f32[2]{0:T(128)S(1)} %get-tuple-element.26, f32[2]{0:T(128)S(1)} %get-tuple-element.25, f32[2]{0:T(128)S(1)} %get-tuple-element.24, f32[2]{0:T(128)S(1)} %get-tuple-element.23), channel_id=1, replica_groups=mesh['sec'=4,'grp'=8] {'sec','grp'}, use_global_device_ids=true, to_apply=%region_7.8 | all-reduce | flops 8 | bytes 64 | tf_op jit(solution)/shard_map/psum | solution.py:147
  212.3 1.9 multiply_add_fusion.2
  218.2 10.9 %all_to_all.94 = f32[8,1,512]{2,1,0:T(1,128)S(1)} all-to-all(f32[8,1,512]{2,1,0:T(1,128)S(1)} %reshape.524), channel_id=1, replica_groups=mesh['sec'=4,'grp'=8] {'grp'}, dimensions={0} | all-to-all | bytes 32768 | tf_op jit(solution)/shard_map/all_to_all | solution.py:134
  232.2 12.4 %psum.181 = f32[2,32,2,2,16]{4,2,0,1,3:T(2,128)} all-reduce(f32[2,32,2,2,16]{4,2,0,1,3:T(2,128)} %copy.152), channel_id=1, replica_groups=mesh['sec'=4,'grp'=8] {'sec'}, use_global_device_ids=true, to_apply=%region_22.23 | all-reduce | flops 4096 | bytes 32768 | tf_op jit(solution)/shard_map/psum | solution.py:139
  251.8 8.9 %all_to_all.95 = f32[8,1,512]{2,1,0:T(1,128)S(1)} all-to-all(f32[8,1,512]{2,1,0:T(1,128)S(1)} %reshape.526), channel_id=1, replica_groups=mesh['sec'=4,'grp'=8] {'grp'}, dimensions={0} | all-to-all | bytes 32768 | tf_op jit(solution)/shard_map/all_to_all | solution.py:143
  264.8 10.1 %psum.182 = f32[2,4,2,2,128]{4,3,2,1,0:T(2,128)S(1)} all-reduce(f32[2,4,2,2,128]{4,3,2,1,0:T(2,128)S(1)} %reshape.487), channel_id=1, replica_groups=mesh['sec'=4,'grp'=8] {'sec'}, use_global_device_ids=true, to_apply=%region_23.24 | all-reduce | flops 4096 | bytes 32768 | tf_op jit(solution)/shard_map/psum | solution.py:144
  275.1 2.2 multiply_reduce_fusion.4
  277.4 38.7 %all-reduce.1 = (f32[2]{0:T(128)S(1)}, f32[2]{0:T(128)S(1)}, f32[2]{0:T(128)S(1)}, f32[2]{0:T(128)S(1)}) all-reduce(f32[2]{0:T(128)S(1)} %get-tuple-element.22, f32[2]{0:T(128)S(1)} %get-tuple-element.21, f32[2]{0:T(128)S(1)} %get-tuple-element.20, f32[2]{0:T(128)S(1)} %get-tuple-element.19), channel_id=1, replica_groups=mesh['sec'=4,'grp'=8] {'sec','grp'}, use_global_device_ids=true, to_apply=%region_17.18 | all-reduce | flops 8 | bytes 64 | tf_op jit(solution)/shard_map/psum | solution.py:147
  316.1 1.9 multiply_add_fusion.1
  322.1 10.9 %all_to_all.96 = f32[8,1,512]{2,1,0:T(1,128)S(1)} all-to-all(f32[8,1,512]{2,1,0:T(1,128)S(1)} %reshape.528), channel_id=1, replica_groups=mesh['sec'=4,'grp'=8] {'grp'}, dimensions={0} | all-to-all | bytes 32768 | tf_op jit(solution)/shard_map/all_to_all | solution.py:134
  336.1 12.4 %psum.187 = f32[2,32,2,2,16]{4,2,0,1,3:T(2,128)} all-reduce(f32[2,32,2,2,16]{4,2,0,1,3:T(2,128)} %copy.162), channel_id=1, replica_groups=mesh['sec'=4,'grp'=8] {'sec'}, use_global_device_ids=true, to_apply=%region_32.33 | all-reduce | flops 4096 | bytes 32768 | tf_op jit(solution)/shard_map/psum | solution.py:139
  355.7 8.9 %all_to_all.97 = f32[8,1,512]{2,1,0:T(1,128)S(1)} all-to-all(f32[8,1,512]{2,1,0:T(1,128)S(1)} %reshape.530), channel_id=1, replica_groups=mesh['sec'=4,'grp'=8] {'grp'}, dimensions={0} | all-to-all | bytes 32768 | tf_op jit(solution)/shard_map/all_to_all | solution.py:143
  368.7 10.1 %psum.188 = f32[2,4,2,2,128]{4,3,2,1,0:T(2,128)S(1)} all-reduce(f32[2,4,2,2,128]{4,3,2,1,0:T(2,128)S(1)} %reshape.492), channel_id=1, replica_groups=mesh['sec'=4,'grp'=8] {'sec'}, use_global_device_ids=true, to_apply=%region_33.34 | all-reduce | flops 4096 | bytes 32768 | tf_op jit(solution)/shard_map/psum | solution.py:144
  378.9 2.2 multiply_reduce_fusion.1
  381.2 38.7 %all-reduce = (f32[2]{0:T(128)S(1)}, f32[2]{0:T(128)S(1)}, f32[2]{0:T(128)S(1)}, f32[2]{0:T(128)S(1)}) all-reduce(f32[2]{0:T(128)S(1)} %get-tuple-element.18, f32[2]{0:T(128)S(1)} %get-tuple-element.17, f32[2]{0:T(128)S(1)} %get-tuple-element.16, f32[2]{0:T(128)S(1)} %get-tuple-element.15), channel_id=1, replica_groups=mesh['sec'=4,'grp'=8] {'sec','grp'}, use_global_device_ids=true, to_apply=%region_27.28 | all-reduce | flops 8 | bytes 64 | tf_op jit(solution)/shard_map/psum | solution.py:147
  (199 shorter events, 78.4 us)
Async XLA Ops:
  0.6 1.9 copy-start
  0.6 12.5 %copy-start.14 = (s32[32]{0:T(128)S(1)}, s32[32]{0:T(128)}, u32[]{:S(2)}) copy-start(s32[32]{0:T(128)} %param.21) | copy-start | bytes 388
  0.7 12.6 %copy-start.15 = (f32[128]{0:T(128)S(1)}, f32[128]{0:T(128)}, u32[]{:S(2)}) copy-start(f32[128]{0:T(128)} %param.20) | copy-start | bytes 1540
  5.8 13.9 %all-to-all-start = ((f32[8,1,512]{2,1,0:T(1,128)}), f32[8,1,512]{2,1,0:T(1,128)S(1)}, u32[]{:S(2)}, u32[]{:S(2)}) async-start(f32[8,1,512]{2,1,0:T(1,128)} %reshape.516), calls=%async_computation | async-start | bytes 32768 | tf_op jit(solution)/shard_map/all_to_all | solution.py:134
  14.6 0.7 copy-start.5
  16.2 31.5 %copy-start.13 = (f32[2,1536]{1,0:T(2,128)S(1)}, f32[2,1536]{1,0:T(2,128)}, u32[]{:S(2)}) copy-start(f32[2,1536]{1,0:T(2,128)} %param.15) | copy-start | bytes 36868
  34.2 4.1 copy-start.1
  42.1 11.1 %all-to-all-start.1 = ((f32[8,1,512]{2,1,0:T(1,128)}), f32[8,1,512]{2,1,0:T(1,128)S(1)}, u32[]{:S(2)}, u32[]{:S(2)}) async-start(f32[8,1,512]{2,1,0:T(1,128)} %reshape.518), calls=%async_computation.1 | async-start | bytes 32768 | tf_op jit(solution)/shard_map/all_to_all | solution.py:143
  110.1 0.7 copy-start.6
  112.4 0.7 copy-start.10
  140.6 3.9 copy-start.2
  214.2 0.7 copy-start.8
  216.5 0.7 copy-start.11
  244.7 3.9 copy-start.3
  318.1 0.7 copy-start.9
  320.4 0.7 copy-start.12
  348.5 3.9 copy-start.4
  352.4 67.5 %copy-start.7 = (f32[2,4,4,1536]{3,2,0,1:T(4,128)S(1)}, f32[2,4,4,1536]{3,2,0,1:T(4,128)}, u32[]{:S(2)}) copy-start(f32[2,4,4,1536]{3,2,0,1:T(4,128)} %copy-done.6) | copy-start | bytes 589828
